TPU v7x, 32 devices: a whole 2x2x4 slice. The times are simulated.
32 devices in a mesh: space: 2 (over x), vel: 16 (over z, y, core).
Axes of the slice: x: 2, y: 2, z: 4, core: 2. Of those that a mesh axis runs over, the one named last changes fastest.
Arguments:
- distribution: float32 [8192, 512], P('vel', 'space'), may hold values from 0.1 to 32, as said below
- normals: float32 [4, 3, 512], P(None, None, 'space'), may hold values from -0.3 to 0.3
- adjacency: int32 [4, 512], P(None, 'space'), may hold values from 0 to 511, as said below
- send_list: int32 [2, 2, 256], P('space'), may hold values from 0 to 255
- block_counts: int32 [2, 2], P(None, 'space'), may hold values from 0 to 2, as said below
Outputs:
- relaxed: float32 [8192, 512], P('vel', 'space')
- fields: float32 [13, 512], P(None, 'space')
Inputs may be any that keep to these rules, and one draw needn't show every extreme that they name: `adjacency`: every entry of 256 or more names a position below 128 times the sum of block_counts over the senders to its group. `block_counts`: no group sends to itself; every other pair has at least one block; one receiving group gets 2 blocks from every other group. `distribution`: Positive.
All inputs are finite; a program needn't handle non-finite values.
Results may differ from a plain program's by a relative error of at most 0.00011.
Values sent between devices are 32-bit elements; how exact they have to be, the bound alone decides.
A program may use at most 64 MiB of HBM per device.

v0:
```python
import jax
import jax.numpy as jnp
from jax import lax
from jax.sharding import PartitionSpec as P

VXY = 32
TILE = 128
ITERS = 2


spacing = 0.3
ellipsoid_mix = -0.25
prandtl = 0.8
visc_power = 0.26
time_step = 0.025


def velocity_nodes(vel_index, z_count):
    comp_x = (vel_index % VXY).astype(jnp.float32)
    comp_y = (vel_index // VXY % VXY).astype(jnp.float32)
    comp_z = (vel_index // (VXY * VXY)).astype(jnp.float32)
    centre = (VXY - 1) / 2.0
    return jnp.stack(
        [
            (comp_x - centre) * spacing,
            (comp_y - centre) * spacing,
            (comp_z - (z_count - 1) / 2.0) * spacing,
        ]
    )


def moment_rows(velocity):
    comp_x, comp_y, comp_z = (velocity[0], velocity[1], velocity[2])
    squared = comp_x * comp_x + comp_y * comp_y + comp_z * comp_z
    return jnp.stack(
        [
            jnp.ones_like(comp_x),
            comp_x,
            comp_y,
            comp_z,
            comp_x * comp_x,
            comp_y * comp_y,
            comp_z * comp_z,
            comp_x * comp_y,
            comp_x * comp_z,
            comp_y * comp_z,
            comp_x * squared,
            comp_y * squared,
            comp_z * squared,
        ]
    )


def quad_rows(velocity):
    comp_x, comp_y, comp_z = (velocity[0], velocity[1], velocity[2])
    return jnp.stack(
        [
            comp_x * comp_x,
            comp_y * comp_y,
            comp_z * comp_z,
            comp_x * comp_y,
            comp_x * comp_z,
            comp_y * comp_z,
            comp_x,
            comp_y,
            comp_z,
            jnp.ones_like(comp_x),
        ]
    )


def macroscopic(moments):
    density = moments[0]
    mean_x = moments[1] / density
    mean_y = moments[2] / density
    mean_z = moments[3] / density
    second = moments[4:10] / density[None, :]
    third = moments[10:13] / density[None, :]
    theta_xx = second[0] - mean_x * mean_x
    theta_yy = second[1] - mean_y * mean_y
    theta_zz = second[2] - mean_z * mean_z
    theta_xy = second[3] - mean_x * mean_y
    theta_xz = second[4] - mean_x * mean_z
    theta_yz = second[5] - mean_y * mean_z
    temper = (theta_xx + theta_yy + theta_zz) / 3.0
    trace_b = second[0] + second[1] + second[2]
    bu_x = second[0] * mean_x + second[3] * mean_y + second[4] * mean_z
    bu_y = second[3] * mean_x + second[1] * mean_y + second[5] * mean_z
    bu_z = second[4] * mean_x + second[5] * mean_y + second[2] * mean_z
    mean_sq = mean_x * mean_x + mean_y * mean_y + mean_z * mean_z
    flux_x = 0.5 * (third[0] - 2.0 * bu_x - mean_x * trace_b + 2.0 * mean_x * mean_sq)
    flux_y = 0.5 * (third[1] - 2.0 * bu_y - mean_y * trace_b + 2.0 * mean_y * mean_sq)
    flux_z = 0.5 * (third[2] - 2.0 * bu_z - mean_z * trace_b + 2.0 * mean_z * mean_sq)
    iso_part = (1.0 - ellipsoid_mix) * temper
    lam_xx = iso_part + ellipsoid_mix * theta_xx
    lam_yy = iso_part + ellipsoid_mix * theta_yy
    lam_zz = iso_part + ellipsoid_mix * theta_zz
    lam_xy = ellipsoid_mix * theta_xy
    lam_xz = ellipsoid_mix * theta_xz
    lam_yz = ellipsoid_mix * theta_yz
    cof_xx = lam_yy * lam_zz - lam_yz * lam_yz
    cof_xy = lam_yz * lam_xz - lam_xy * lam_zz
    cof_xz = lam_xy * lam_yz - lam_yy * lam_xz
    cof_yy = lam_xx * lam_zz - lam_xz * lam_xz
    cof_yz = lam_xy * lam_xz - lam_xx * lam_yz
    cof_zz = lam_xx * lam_yy - lam_xy * lam_xy
    determinant = lam_xx * cof_xx + lam_xy * cof_xy + lam_xz * cof_xz
    inv_xx = cof_xx / determinant
    inv_yy = cof_yy / determinant
    inv_zz = cof_zz / determinant
    inv_xy = cof_xy / determinant
    inv_xz = cof_xz / determinant
    inv_yz = cof_yz / determinant
    lin_x = inv_xx * mean_x + inv_xy * mean_y + inv_xz * mean_z
    lin_y = inv_xy * mean_x + inv_yy * mean_y + inv_yz * mean_z
    lin_z = inv_xz * mean_x + inv_yz * mean_y + inv_zz * mean_z
    offset = mean_x * lin_x + mean_y * lin_y + mean_z * lin_z
    collide = prandtl * density * jnp.exp(visc_power * jnp.log(temper))
    return jnp.stack(
        [
            density,
            mean_x,
            mean_y,
            mean_z,
            theta_xx,
            theta_yy,
            theta_zz,
            theta_xy,
            theta_xz,
            theta_yz,
            flux_x,
            flux_y,
            flux_z,
            inv_xx,
            inv_yy,
            inv_zz,
            2.0 * inv_xy,
            2.0 * inv_xz,
            2.0 * inv_yz,
            -2.0 * lin_x,
            -2.0 * lin_y,
            -2.0 * lin_z,
            offset,
            collide,
        ]
    )


def ghost_slots(adjacency, counts, cells, groups, slot_count):
    ends = jnp.cumsum(counts) * TILE
    starts = ends - counts * TILE
    is_local = adjacency < cells
    position = jnp.maximum(adjacency - cells, 0)
    source = jnp.sum((ends[:, None, None] <= position[None]).astype(jnp.int32), axis=0)
    source = jnp.minimum(source, groups - 1)
    group_ids = jnp.arange(groups, dtype=jnp.int32)[:, None, None]
    chosen = jnp.sum(jnp.where(group_ids == source[None], starts[:, None, None], 0), axis=0)
    slot_pos = jnp.clip(position - chosen, 0, slot_count - 1)
    return (is_local, source, slot_pos)


def relax(current, neighbours, velocity, normals, params, norm_z, equilibrium):
    gauss = params[0][None, :] * equilibrium / norm_z[None, :]
    outflow = jnp.zeros(current.shape, jnp.float32)
    inflow = jnp.zeros(current.shape, jnp.float32)
    for side in range(normals.shape[0]):
        normal_speed = (
            velocity[0][:, None] * normals[side, 0][None, :]
            + velocity[1][:, None] * normals[side, 1][None, :]
            + velocity[2][:, None] * normals[side, 2][None, :]
        )
        outflow = outflow + jnp.maximum(normal_speed, 0.0)
        inflow = inflow + jnp.minimum(normal_speed, 0.0) * neighbours[side]
    return current + time_step * (
        params[23][None, :] * (gauss - current) - outflow * current - inflow
    )


def per_device(distribution, normals, adjacency, send_list, block_counts):
    vel_local = distribution.shape[0]
    cells = distribution.shape[1]
    total_vel = vel_local * lax.axis_size("vel")
    z_count = total_vel // (VXY * VXY)
    groups = send_list.shape[1]
    slot_count = send_list.shape[2]
    vel_index = lax.axis_index("vel") * vel_local + jnp.arange(vel_local, dtype=jnp.int32)
    velocity = velocity_nodes(vel_index, z_count)
    moment_table = moment_rows(velocity)
    quad_table = quad_rows(velocity).T
    is_local, source, slot_pos = ghost_slots(
        adjacency, block_counts[:, 0], cells, groups, slot_count
    )
    ghost_index = source * slot_count + slot_pos
    local_index = jnp.where(is_local, adjacency, 0)
    send_rows = send_list[0].reshape(-1)

    def reduce_moments(current):
        partial_value = (
            jnp.dot(
                moment_table,
                current,
                precision=lax.Precision.HIGHEST,
                preferred_element_type=jnp.float32,
            )
            / total_vel
        )
        return macroscopic(lax.psum(partial_value, "vel"))

    current = distribution
    for iteration in range(ITERS):
        params = reduce_moments(current)
        ghosts = lax.all_to_all(
            jnp.take(current, send_rows, axis=1), "space", split_axis=1, concat_axis=1, tiled=True
        )
        exponent = jnp.dot(
            quad_table,
            params[13:23],
            precision=lax.Precision.HIGHEST,
            preferred_element_type=jnp.float32,
        )
        equilibrium = jnp.exp(-0.5 * exponent)
        norm_z = lax.psum(jnp.sum(equilibrium, axis=0) / total_vel, "vel")
        neighbours = [
            jnp.where(
                is_local[side][None, :],
                jnp.take(current, local_index[side], axis=1),
                jnp.take(ghosts, ghost_index[side], axis=1),
            )
            for side in range(normals.shape[0])
        ]
        current = relax(current, neighbours, velocity, normals, params, norm_z, equilibrium)
    final = reduce_moments(current)
    return (current, final[:13])


def solution(mesh):
    placed = (
        P("vel", "space"),
        P(None, None, "space"),
        P(None, "space"),
        P("space", None, None),
        P(None, "space"),
    )
    return jax.shard_map(
        per_device,
        mesh=mesh,
        in_specs=placed,
        out_specs=(P("vel", "space"), P(None, "space")),
        check_vma=False,
    )
```

profile of v0, /device:TPU:0, one launch (start us, length us, event | category | flops | bytes accessed | tf_op | source)
XLA Modules:
  0.0 309.6 jit_solution(3086310342836148335)
XLA Ops:
  1.3 1.2 copy.33
  2.6 1.6 gather_fusion.1
  4.2 1.1 broadcast_select_fusion.1
  5.4 4.4 %all-to-all-start = ((f32[512,2,256]{0,2,1:T(8,128)}), f32[512,2,256]{0,2,1:T(8,128)S(1)}, u32[]{:S(2)}, u32[]{:S(2)}) async-start(f32[512,2,256]{0,2,1:T(8,128)} %bitcast.20), calls=%async_computation | async-start | bytes 2097152 | tf_op jit(solution)/shard_map/all_to_all | solution.py:212
  11.7 62.4 %psum.35 = f32[13,256]{1,0:T(8,128)S(1)} all-reduce(f32[13,256]{1,0:T(8,128)S(1)} %convolution_multiply_fusion.4), channel_id=1, replica_groups=mesh['space'=2,'vel'=16] {'vel'}, use_global_device_ids=true, to_apply=%region_0.1 | all-reduce | flops 3328 | bytes 26624 | tf_op jit(solution)/shard_map/psum | solution.py:207
  74.9 29.5 %psum.36 = f32[256]{0:T(256)S(1)} all-reduce(f32[256]{0:T(256)S(1)} %broadcast_multiply_fusion.1), channel_id=1, replica_groups=mesh['space'=2,'vel'=16] {'vel'}, use_global_device_ids=true, to_apply=%region_2.3 | all-reduce | flops 256 | bytes 2048 | tf_op jit(solution)/shard_map/psum | solution.py:222
  104.5 1.8 gather_fusion
  106.2 1.2 copy.34
  107.5 1.8 gather_fusion.3
  109.3 2.0 copy.38
  111.3 1.8 gather_fusion.5
  113.1 2.1 copy.41
  115.1 1.8 gather_fusion.7
  116.9 2.1 copy.44
  125.0 1.8 gather_fusion.8
  126.7 2.1 copy.45
  128.9 2.9 fusion.16
  132.3 57.6 %psum.37 = f32[13,256]{1,0:T(8,128)S(1)} all-reduce(f32[13,256]{1,0:T(8,128)S(1)} %convolution_multiply_fusion.3), channel_id=1, replica_groups=mesh['space'=2,'vel'=16] {'vel'}, use_global_device_ids=true, to_apply=%region_6.10 | all-reduce | flops 3328 | bytes 26624 | tf_op jit(solution)/shard_map/psum | solution.py:207
  190.1 1.6 gather_fusion.10
  191.7 1.1 broadcast_select_fusion
  192.9 3.8 %all-to-all-start.1 = ((f32[512,2,256]{0,2,1:T(8,128)}), f32[512,2,256]{0,2,1:T(8,128)S(1)}, u32[]{:S(2)}, u32[]{:S(2)}) async-start(f32[512,2,256]{0,2,1:T(8,128)} %bitcast.39), calls=%async_computation.1 | async-start | bytes 2097152 | tf_op jit(solution)/shard_map/all_to_all | solution.py:212
  198.6 1.8 gather_fusion.14
  200.4 1.8 gather_fusion.16
  202.6 2.1 copy.54
  205.7 1.4 fusion.95
  207.2 29.5 %psum.38 = f32[256]{0:T(256)S(1)} all-reduce(f32[256]{0:T(256)S(1)} %broadcast_multiply_fusion), channel_id=1, replica_groups=mesh['space'=2,'vel'=16] {'vel'}, use_global_device_ids=true, to_apply=%region_8.12 | all-reduce | flops 256 | bytes 2048 | tf_op jit(solution)/shard_map/psum | solution.py:222
  237.6 1.8 gather_fusion.13
  239.4 1.8 gather_fusion.15
  241.2 1.8 gather_fusion.17
  247.4 2.9 fusion.6
  250.7 57.7 %psum.39 = f32[13,256]{1,0:T(8,128)S(1)} all-reduce(f32[13,256]{1,0:T(8,128)S(1)} %convolution_multiply_fusion.2), channel_id=1, replica_groups=mesh['space'=2,'vel'=16] {'vel'}, use_global_device_ids=true, to_apply=%region_9.13 | all-reduce | flops 3328 | bytes 26624 | tf_op jit(solution)/shard_map/psum | solution.py:207
  308.4 1.2 stack.14
  (131 shorter events, 19.2 us)
Async XLA Ops:
  5.3 6.0 %copy-start = (f32[512,256]{1,0:T(8,128)S(1)}, f32[512,256]{1,0:T(8,128)}, u32[]{:S(2)}) copy-start(f32[512,256]{1,0:T(8,128)} %param.11) | copy-start | bytes 1572868
  5.4 113.7 %all-to-all-start = ((f32[512,2,256]{0,2,1:T(8,128)}), f32[512,2,256]{0,2,1:T(8,128)S(1)}, u32[]{:S(2)}, u32[]{:S(2)}) async-start(f32[512,2,256]{0,2,1:T(8,128)} %bitcast.20), calls=%async_computation | async-start | bytes 2097152 | tf_op jit(solution)/shard_map/all_to_all | solution.py:212
  10.0 0.7 copy-start.12
  10.0 0.8 copy-start.10
  116.9 2.1 copy-start.11
  126.7 2.1 copy-start.4
  126.7 2.1 copy-start.5
  192.9 43.8 %all-to-all-start.1 = ((f32[512,2,256]{0,2,1:T(8,128)}), f32[512,2,256]{0,2,1:T(8,128)S(1)}, u32[]{:S(2)}, u32[]{:S(2)}) async-start(f32[512,2,256]{0,2,1:T(8,128)} %bitcast.39), calls=%async_computation.1 | async-start | bytes 2097152 | tf_op jit(solution)/shard_map/all_to_all | solution.py:212
  202.5 2.1 copy-start.6
  242.9 1.0 copy-start.7
  244.0 1.0 copy-start.8
  245.0 1.0 copy-start.9
  246.1 1.0 copy-start.2
  246.1 1.4 copy-start.3
  250.4 59.3 %copy-start.1 = (f32[512,256]{1,0:T(8,128)}, f32[512,256]{1,0:T(8,128)S(1)}, u32[]{:S(2)}) copy-start(f32[512,256]{1,0:T(8,128)S(1)} %fusion.6) | copy-start | bytes 1572868
where the time goes:
time: 311 us; the launch traced here: 310 us
  blocking collectives  237 us (76%)
  local copies, waits for them, and re-layouts  51.6 us (17%)
  other arithmetic  9.24 us (3%)
  starting transfers between devices  8.12 us (3%)
    psum x3, blocking collectives, reduce_moments(): return macroscopic(lax.psum(partial_value, 'vel'))  178 us
    psum x2, blocking collectives, per_device(): norm_z = lax.psum(jnp.sum(equilibrium, axis=0) / total_vel, 'vel')  59 us
    gather x16, local copies, waits for them, and re-layouts, per_device(): jnp.take(current, local_index[side], axis=1)  23.4 us
    gather x16, local copies, waits for them, and re-layouts, per_device(): jnp.take(ghosts, ghost_index[side], axis=1)  20.1 us
    all_to_all x2, starting transfers between devices, per_device(): lax.all_to_all(jnp.take(current, send_rows, axis=1), 'space', split_axis=...  8.12 us
  transfers between devices with their start and end apart: 2, of which 0 were waited for; matrix products, arithmetic and copies ran while one was open for 9% of the time, Pallas kernels for 0%

commit v1 on v0

--- a/solution.py
+++ b/solution.py
@@ -1,6 +1,10 @@
+import functools
+
 import jax
 import jax.numpy as jnp
 from jax import lax
+from jax.experimental import pallas as pl
+from jax.experimental.pallas import tpu as pltpu
 from jax.sharding import PartitionSpec as P
 
 VXY = 32
@@ -233,6 +237,453 @@
     return (current, final[:13])
 
 
+MESH = pl.DeviceIdType.MESH
+LOG2E = 1.4426950408889634
+QUAD = 4
+CHUNKS = 4
+HI = lax.Precision.HIGHEST
+
+
+def coefficient_rows(m):
+    full = macroscopic_rows([m[r : r + 1, :] for r in range(13)])
+    scale = -0.5 * LOG2E
+    return full[:13], [row * scale for row in full[13:23]], full[23]
+
+
+def macroscopic_rows(m):
+    density = m[0]
+    inv_d = 1.0 / density
+    ux, uy, uz = (m[1] * inv_d, m[2] * inv_d, m[3] * inv_d)
+    b = [m[r] * inv_d for r in range(4, 10)]
+    third = [m[r] * inv_d for r in range(10, 13)]
+    txx, tyy, tzz = (b[0] - ux * ux, b[1] - uy * uy, b[2] - uz * uz)
+    txy, txz, tyz = (b[3] - ux * uy, b[4] - ux * uz, b[5] - uy * uz)
+    temper = (txx + tyy + tzz) * (1.0 / 3.0)
+    trace_b = b[0] + b[1] + b[2]
+    bux = b[0] * ux + b[3] * uy + b[4] * uz
+    buy = b[3] * ux + b[1] * uy + b[5] * uz
+    buz = b[4] * ux + b[5] * uy + b[2] * uz
+    usq = ux * ux + uy * uy + uz * uz
+    qx = 0.5 * (third[0] - 2.0 * bux - ux * trace_b + 2.0 * ux * usq)
+    qy = 0.5 * (third[1] - 2.0 * buy - uy * trace_b + 2.0 * uy * usq)
+    qz = 0.5 * (third[2] - 2.0 * buz - uz * trace_b + 2.0 * uz * usq)
+    iso = (1.0 - ellipsoid_mix) * temper
+    lxx, lyy, lzz = (iso + ellipsoid_mix * txx, iso + ellipsoid_mix * tyy, iso + ellipsoid_mix * tzz)
+    lxy, lxz, lyz = (ellipsoid_mix * txy, ellipsoid_mix * txz, ellipsoid_mix * tyz)
+    cxx = lyy * lzz - lyz * lyz
+    cxy = lyz * lxz - lxy * lzz
+    cxz = lxy * lyz - lyy * lxz
+    cyy = lxx * lzz - lxz * lxz
+    cyz = lxy * lxz - lxx * lyz
+    czz = lxx * lyy - lxy * lxy
+    inv_det = 1.0 / (lxx * cxx + lxy * cxy + lxz * cxz)
+    ixx, iyy, izz = (cxx * inv_det, cyy * inv_det, czz * inv_det)
+    ixy, ixz, iyz = (cxy * inv_det, cxz * inv_det, cyz * inv_det)
+    wx = ixx * ux + ixy * uy + ixz * uz
+    wy = ixy * ux + iyy * uy + iyz * uz
+    wz = ixz * ux + iyz * uy + izz * uz
+    offset = ux * wx + uy * wy + uz * wz
+    collide = prandtl * density * jnp.exp(visc_power * jnp.log(temper))
+    return [
+        density, ux, uy, uz, txx, tyy, tzz, txy, txz, tyz, qx, qy, qz,
+        ixx, iyy, izz, 2.0 * ixy, 2.0 * ixz, 2.0 * iyz,
+        -2.0 * wx, -2.0 * wy, -2.0 * wz, offset, collide,
+    ]
+
+
+def node_velocity(index, z_count):
+    shift = VXY.bit_length() - 1
+    centre = (VXY - 1) / 2.0
+    vx = ((index & (VXY - 1)).astype(jnp.float32) - centre) * spacing
+    vy = (((index >> shift) & (VXY - 1)).astype(jnp.float32) - centre) * spacing
+    vz = ((index >> (2 * shift)).astype(jnp.float32) - (z_count - 1) / 2.0) * spacing
+    return vx, vy, vz
+
+
+def exponent_at(q, vx, vy, vz):
+    return (
+        vx * (q[0] * vx + q[3] * vy + q[4] * vz + q[6])
+        + vy * (q[1] * vy + q[5] * vz + q[7])
+        + (vz * (q[2] * vz + q[8]) + q[9])
+    )
+
+
+def x_column(width):
+    rows = lax.broadcasted_iota(jnp.int32, (VXY, width), 0)
+    return (rows.astype(jnp.float32) - (VXY - 1) / 2.0) * spacing
+
+
+def gauss_total(q, width, z_count):
+    vx = x_column(width)
+    base = (q[0] * vx + q[6]) * vx
+
+    def level(k, acc):
+        vz = (k.astype(jnp.float32) - (z_count - 1) / 2.0) * spacing
+        slope = q[4] * vz
+        odd = q[5] * vz + q[7]
+        even = vz * (q[2] * vz + q[8]) + q[9]
+        level_base = base + vx * slope + even
+        for j in range(VXY // 2):
+            vy = (j + 0.5) * spacing
+            mid = level_base + q[1] * (vy * vy)
+            tilt = (vx * q[3] + odd) * vy
+            acc = acc + (jnp.exp2(mid + tilt) + jnp.exp2(mid - tilt))
+        return acc
+
+    acc = lax.fori_loop(0, z_count, level, jnp.zeros((VXY, width), jnp.float32))
+    return jnp.sum(acc, axis=0, keepdims=True)
+
+
+def gauss_moments(q, width, z_count):
+    vx = x_column(width)
+    base = (q[0] * vx + q[6]) * vx
+    zero = jnp.zeros((VXY, width), jnp.float32)
+
+    def level(k, carry):
+        vz = (k.astype(jnp.float32) - (z_count - 1) / 2.0) * spacing
+        slope = q[4] * vz
+        odd = q[5] * vz + q[7]
+        even = vz * (q[2] * vz + q[8]) + q[9]
+        level_base = base + vx * slope + even
+        s0, s1, s2, s3 = (zero, zero, zero, zero)
+        for j in range(VXY // 2):
+            vy = (j + 0.5) * spacing
+            mid = level_base + q[1] * (vy * vy)
+            tilt = (vx * q[3] + odd) * vy
+            up = jnp.exp2(mid + tilt)
+            down = jnp.exp2(mid - tilt)
+            both = up + down
+            diff = (up - down) * vy
+            s0 = s0 + both
+            s1 = s1 + diff
+            s2 = s2 + both * (vy * vy)
+            s3 = s3 + diff * (vy * vy)
+        z0 = vz * s0
+        zz0 = vz * z0
+        z1 = vz * s1
+        new = (s0, s1, s2, s3, z0, zz0, z1, vz * zz0 + vz * s2, vz * z1)
+        return tuple(a + b for a, b in zip(carry, new))
+
+    s0, s1, s2, s3, z0, zz0, z1, zc, zz1 = lax.fori_loop(0, z_count, level, (zero,) * 9)
+    vxx = vx * vx
+    terms = [
+        s0, vx * s0, s1, z0, vxx * s0, s2, zz0, vx * s1, vx * z0, z1,
+        vx * (vxx * s0 + s2 + zz0), vxx * s1 + s3 + zz1, vxx * z0 + zc,
+    ]
+    return [jnp.sum(t, axis=0, keepdims=True) for t in terms]
+
+
+def split_dot(lhs, rhs):
+    return jnp.dot(lhs, rhs, precision=HI, preferred_element_type=jnp.float32)
+
+
+def step_kernel(
+    total_vel,
+    f_ref, n_ref, adj_ref, send_ref,
+    out_ref, fields_ref,
+    fx, nx, adjx, sendx, oh, tr0, fnew, tr1, phi_ref,
+    part0, rs0, zb0, full0, part1, rs1, zb1, full1,
+    bulk_s, bulk_r, meta_s, meta_r,
+    a_s, a_r, b_s, b_r, c_s, c_r,
+    d_s, d_r, e_s, e_r, g_s, g_r,
+):
+    nodes, cells = f_ref.shape
+    both = 2 * cells
+    faces = n_ref.shape[0]
+    z_count = total_vel // (VXY * VXY)
+    rows = nodes // CHUNKS
+    group = lax.axis_index("space")
+    other = 1 - group
+    vel = lax.axis_index("vel")
+    ring = total_vel // nodes // QUAD
+    me_q = lax.rem(vel, QUAD)
+    me_z = vel // QUAD
+
+    def at(space, z, q):
+        return (space, z * QUAD + q)
+
+    def q_of(step):
+        return lax.rem(me_q + step, QUAD)
+
+    def z_of(step):
+        return lax.rem(me_z + step, ring)
+
+    barrier = pltpu.get_barrier_semaphore()
+    for step in range(1, QUAD):
+        pl.semaphore_signal(barrier, inc=1, device_id=at(group, me_z, q_of(step)), device_id_type=MESH)
+    for step in range(1, ring):
+        pl.semaphore_signal(barrier, inc=1, device_id=at(group, z_of(step), me_q), device_id_type=MESH)
+    for step in range(QUAD):
+        pl.semaphore_signal(barrier, inc=1, device_id=at(other, me_z, q_of(step)), device_id_type=MESH)
+
+    lane_v = node_velocity(lax.broadcasted_iota(jnp.int32, (1, nodes), 1) + vel * nodes, z_count)
+    lx, ly, lz = lane_v
+    sq = lx * lx + ly * ly + lz * lz
+    table = [
+        jnp.ones_like(lx), lx, ly, lz, lx * lx, ly * ly, lz * lz,
+        lx * ly, lx * lz, ly * lz, lx * sq, ly * sq, lz * sq,
+    ]
+    row_id = lax.broadcasted_iota(jnp.int32, (16, nodes), 0)
+    phi = jnp.zeros((16, nodes), jnp.float32)
+    for r, row in enumerate(table):
+        phi = jnp.where(row_id == r, row, phi)
+    phi_ref[...] = phi
+    inv_total = 1.0 / total_vel
+    half = cells // 2
+    m_part = split_dot(phi, f_ref[...]) * inv_total
+    for q in range(QUAD):
+        part0[q] = m_part[(q // 2) * 8 : (q // 2) * 8 + 8, (q % 2) * half : (q % 2 + 1) * half]
+
+    pl.semaphore_wait(barrier, 2 * QUAD - 1 + ring - 1)
+
+    def remote(src, dst, s, r, dev):
+        return pltpu.make_async_remote_copy(
+            src_ref=src, dst_ref=dst, send_sem=s, recv_sem=r, device_id=dev, device_id_type=MESH
+        )
+
+    pair = at(other, me_z, me_q)
+    metas = [
+        remote(send_ref, sendx, meta_s.at[0], meta_r.at[0], pair),
+        remote(adj_ref, adjx, meta_s.at[1], meta_r.at[1], pair),
+        remote(n_ref, nx, meta_s.at[2], meta_r.at[2], pair),
+    ]
+    for copy in metas:
+        copy.start()
+
+    def scatter(part, rs, s, r):
+        copies = [
+            remote(part.at[q_of(t)], rs.at[t], s.at[t], r.at[t], at(group, me_z, q_of(t)))
+            for t in range(1, QUAD)
+        ]
+        for copy in copies:
+            copy.start()
+        return copies
+
+    def along_z(zb, s, r):
+        copies = [
+            remote(zb.at[0], zb.at[t], s.at[t], r.at[t], at(group, z_of(t), me_q))
+            for t in range(1, ring)
+        ]
+        for copy in copies:
+            copy.start()
+        return copies
+
+    def bulk(c):
+        part = pl.ds(pl.multiple_of(c * rows, rows), rows)
+        return remote(f_ref.at[part], fx.at[part], bulk_s.at[c], bulk_r.at[c], pair)
+
+    first = scatter(part0, rs0, a_s, a_r)
+    for c in range(CHUNKS):
+        bulk(c).start()
+
+    for copy in metas:
+        copy.wait_recv()
+    slot_id = lax.broadcasted_iota(jnp.int32, (cells, cells), 0)
+    cell_id = lax.broadcasted_iota(jnp.int32, (both, both), 0)
+
+    def listed(send_row, adjacency):
+        hit = (slot_id == adjacency - cells).astype(jnp.bfloat16)
+        values = jnp.broadcast_to(send_row, (8, cells)).astype(jnp.float32).astype(jnp.bfloat16)
+        got = jnp.dot(values, hit, preferred_element_type=jnp.float32)
+        return got[0:1].astype(jnp.int32)
+
+    to_me = sendx[0, pl.ds(group, 1), :]
+    to_other = send_ref[0, pl.ds(other, 1), :]
+    for k in range(faces):
+        own = adj_ref[k : k + 1, :]
+        theirs = adjx[k : k + 1, :]
+        own = jnp.where(own < cells, own, cells + listed(to_me, own))
+        theirs = jnp.where(theirs < cells, cells + theirs, listed(to_other, theirs))
+        index = jnp.concatenate([own, theirs], axis=1)
+        oh[k] = (cell_id == index).astype(jnp.bfloat16)
+
+    for copy in first:
+        copy.wait_recv()
+    zb0[0] = part0[me_q] + rs0[1] + rs0[2] + rs0[3]
+    second = along_z(zb0, b_s, b_r)
+    for copy in second:
+        copy.wait_recv()
+    total0 = zb0[0]
+    for t in range(1, ring):
+        total0 = total0 + zb0[t]
+    full0[0, me_q] = total0
+    third = []
+    for t in range(1, QUAD):
+        third.append(
+            remote(full0.at[0, me_q], full0.at[0, me_q], c_s.at[t], c_r.at[t], at(group, me_z, q_of(t)))
+        )
+    for t in range(QUAD):
+        third.append(
+            remote(
+                full0.at[0, me_q], full0.at[1, me_q], c_s.at[QUAD + t], c_r.at[QUAD + t],
+                at(other, me_z, q_of(t)),
+            )
+        )
+    for copy in third:
+        copy.start()
+
+    def local_velocity(c, width):
+        index = lax.broadcasted_iota(jnp.int32, (rows, width), 0) + (vel * nodes + c * rows)
+        return node_velocity(index, z_count)
+
+    def transport(state, c, width):
+        high = state.astype(jnp.bfloat16)
+        low = (state - high.astype(jnp.float32)).astype(jnp.bfloat16)
+        lhs = jnp.concatenate([high, low], axis=0)
+        vx, vy, vz = local_velocity(c, width)
+        mine = state[:, :width]
+        result = jnp.zeros((rows, width), jnp.float32)
+        for k in range(faces):
+            got = jnp.dot(lhs, oh[k, :, 0:width], preferred_element_type=jnp.float32)
+            got = got[:rows] + got[rows:]
+            normal = []
+            for d in range(3):
+                line = n_ref[k, d : d + 1, :]
+                if width > cells:
+                    line = jnp.concatenate([line, nx[k, d : d + 1, :]], axis=1)
+                normal.append(line)
+            speed = vx * normal[0] + vy * normal[1] + vz * normal[2]
+            result = result + (jnp.maximum(speed, 0.0) * mine + jnp.minimum(speed, 0.0) * got)
+        return result
+
+    def wide(c):
+        part = pl.ds(pl.multiple_of(c * rows, rows), rows)
+        return part, jnp.concatenate([f_ref[part, :], fx[part, :]], axis=1)
+
+    def first_transport(c, carry):
+        bulk(c).wait_recv()
+        part, state = wide(c)
+        tr0[part, :] = transport(state, c, both)
+        return carry
+
+    early = CHUNKS // 2
+    lax.fori_loop(0, early, first_transport, 0)
+    for copy in third:
+        copy.wait_recv()
+
+    def joined(full):
+        top = jnp.concatenate([full[0], full[1]], axis=1)
+        bottom = jnp.concatenate([full[2], full[3]], axis=1)
+        return jnp.concatenate([top, bottom], axis=0)
+
+    mom0 = jnp.concatenate([joined(full0[0]), joined(full0[1])], axis=1)
+    fields0, quad0, freq0 = coefficient_rows(mom0)
+    z0 = gauss_total(quad0, both, z_count) * inv_total
+    gain0 = time_step * freq0 * fields0[0] / z0
+    keep0 = 1.0 - time_step * freq0
+
+    lax.fori_loop(early, CHUNKS, first_transport, 0)
+
+    def second_transport(c, carry):
+        part, state = wide(c)
+        vx, vy, vz = local_velocity(c, both)
+        state = keep0 * state - time_step * tr0[part, :] + gain0 * jnp.exp2(exponent_at(quad0, vx, vy, vz))
+        fnew[part, :] = state[:, :cells]
+        tr1[part, :] = transport(state, c, cells)
+        return carry
+
+    lax.fori_loop(0, CHUNKS, second_transport, 0)
+
+    phi = phi_ref[...]
+    m_new = split_dot(phi, fnew[...]) * inv_total
+    m_tr = split_dot(phi, tr1[...]) * inv_total
+    for q in range(QUAD):
+        src = m_new if q < 2 else m_tr
+        part1[q] = src[:, (q % 2) * half : (q % 2 + 1) * half]
+    fourth = scatter(part1, rs1, d_s, d_r)
+    for copy in fourth:
+        copy.wait_recv()
+    zb1[0] = part1[me_q] + rs1[1] + rs1[2] + rs1[3]
+    fifth = along_z(zb1, e_s, e_r)
+    for copy in fifth:
+        copy.wait_recv()
+    total1 = zb1[0]
+    for t in range(1, ring):
+        total1 = total1 + zb1[t]
+    full1[me_q] = total1
+    sixth = [
+        remote(full1.at[me_q], full1.at[me_q], g_s.at[t], g_r.at[t], at(group, me_z, q_of(t)))
+        for t in range(1, QUAD)
+    ]
+    for copy in sixth:
+        copy.start()
+    for copy in sixth:
+        copy.wait_recv()
+    mom1 = jnp.concatenate([full1[0], full1[1]], axis=1)
+    mom_t = jnp.concatenate([full1[2], full1[3]], axis=1)
+    fields1, quad1, freq1 = coefficient_rows(mom1)
+    sums = gauss_moments(quad1, cells, z_count)
+    inv_sum = 1.0 / sums[0]
+    lift = time_step * freq1 * fields1[0]
+    gain1 = lift * inv_sum * float(total_vel)
+    keep1 = 1.0 - time_step * freq1
+
+    def finish(c, carry):
+        part = pl.ds(pl.multiple_of(c * rows, rows), rows)
+        vx, vy, vz = local_velocity(c, cells)
+        out_ref[part, :] = (
+            keep1 * fnew[part, :] - time_step * tr1[part, :]
+            + gain1 * jnp.exp2(exponent_at(quad1, vx, vy, vz))
+        )
+        return carry
+
+    lax.fori_loop(0, CHUNKS, finish, 0)
+    ratio = lift * inv_sum
+    last = [
+        keep1 * mom1[r : r + 1] - time_step * mom_t[r : r + 1] + ratio * sums[r] for r in range(13)
+    ]
+    final = macroscopic_rows(last)
+    for r in range(13):
+        fields_ref[r : r + 1, :] = final[r]
+    for c in range(CHUNKS):
+        bulk(c).wait_send()
+    for copy in metas + first + second + third + fourth + fifth + sixth:
+        copy.wait_send()
+
+
+def per_device_pair(distribution, normals, adjacency, send_list, block_counts):
+    nodes, cells = distribution.shape
+    size = lax.axis_size("vel")
+    ring = size // QUAD
+    half = cells // 2
+    f32 = jnp.float32
+    dma = pltpu.SemaphoreType.DMA
+    vmem = pl.BlockSpec(memory_space=pltpu.VMEM)
+    return pl.pallas_call(
+        functools.partial(step_kernel, nodes * size),
+        out_shape=(
+            jax.ShapeDtypeStruct((nodes, cells), f32),
+            jax.ShapeDtypeStruct((13, cells), f32),
+        ),
+        in_specs=[vmem] * 4,
+        out_specs=(vmem, vmem),
+        scratch_shapes=[
+            pltpu.VMEM((nodes, cells), f32),
+            pltpu.VMEM(normals.shape, f32),
+            pltpu.VMEM(adjacency.shape, jnp.int32),
+            pltpu.VMEM(send_list.shape, jnp.int32),
+            pltpu.VMEM((normals.shape[0], 2 * cells, 2 * cells), jnp.bfloat16),
+            pltpu.VMEM((nodes, 2 * cells), f32),
+            pltpu.VMEM((nodes, cells), f32),
+            pltpu.VMEM((nodes, cells), f32),
+            pltpu.VMEM((16, nodes), f32),
+            pltpu.VMEM((QUAD, 8, half), f32),
+            pltpu.VMEM((QUAD, 8, half), f32),
+            pltpu.VMEM((ring, 8, half), f32),
+            pltpu.VMEM((2, QUAD, 8, half), f32),
+            pltpu.VMEM((QUAD, 16, half), f32),
+            pltpu.VMEM((QUAD, 16, half), f32),
+            pltpu.VMEM((ring, 16, half), f32),
+            pltpu.VMEM((QUAD, 16, half), f32),
+            dma((CHUNKS,)), dma((CHUNKS,)), dma((3,)), dma((3,)),
+            dma((QUAD,)), dma((QUAD,)), dma((ring,)), dma((ring,)), dma((2 * QUAD,)), dma((2 * QUAD,)),
+            dma((QUAD,)), dma((QUAD,)), dma((ring,)), dma((ring,)), dma((QUAD,)), dma((QUAD,)),
+        ],
+        compiler_params=pltpu.CompilerParams(collective_id=0, has_side_effects=True),
+        name="steps",
+    )(distribution, normals, adjacency, send_list)
+
+
 def solution(mesh):
     placed = (
         P("vel", "space"),
@@ -241,8 +692,9 @@
         P("space", None, None),
         P(None, "space"),
     )
+    pair = mesh.shape["space"] == 2 and mesh.shape["vel"] % QUAD == 0 and ITERS == 2
     return jax.shard_map(
-        per_device,
+        per_device_pair if pair else per_device,
         mesh=mesh,
         in_specs=placed,
         out_specs=(P("vel", "space"), P(None, "space")),

time: 311 us -> 46.5 us (0.15)
  blocking collectives: 237 us -> 0 us
  local copies, waits for them, and re-layouts: 51.6 us -> 3.8 us
  Pallas kernels: 0 us -> 41.8 us
  other arithmetic: 9.24 us -> 0 us
  starting transfers between devices: 8.12 us -> 0 us
    psum x5 -> x0, blocking collectives: 237 us -> none  [the longest x3 178 us: reduce_moments(): return macroscopic(lax.psum(partial_value, 'vel'))]
    gather x34 -> x0, local copies, waits for them, and re-layouts: 46.8 us -> none  [the longest x16 23.4 us: per_device(): jnp.take(current, local_index[side], axis=1)]
    pallas_call x0 -> x1, Pallas kernels: none -> 41.8 us  [per_device_pair(): pl.pallas_call(functools.partial(step_kernel, nodes * size), out_shape=(j...]
    all_to_all x2 -> x0, starting transfers between devices: 8.12 us -> none  [per_device(): lax.all_to_all(jnp.take(current, send_rows, axis=1), 'space', split_axis=...]
    add x6 -> x0, other arithmetic: 5.96 us -> none  [the longest x2 5.86 us: relax(): current + time_step * (params[23][None, :] * (gauss - current) - outflow...]
  transfers between devices with their start and end apart: 2 -> 0, of which waited for: 0 -> 0; matrix products, arithmetic and copies ran while one was open for 9% -> 0% of each run, Pallas kernels for 0% -> 0%
where the time goes in v1:
time: 46.5 us; the launch traced here: 46.3 us
  Pallas kernels  41.8 us (90%)
  local copies, waits for them, and re-layouts  3.8 us (8%)
  between operations  0.65 us (1%)
    pallas_call x1, Pallas kernels, per_device_pair(): pl.pallas_call(functools.partial(step_kernel, nodes * size), out_shape=(j...  41.8 us
    unnamed x5, local copies, waits for them, and re-layouts  3.8 us

profile of v1, /device:TPU:0, one launch (start us, length us, event | category | flops | bytes accessed | tf_op | source)
XLA Modules:
  0.0 46.3 jit_solution(14038214620277086757)
XLA Ops:
  0.6 1.3 %copy.6.n_ref = f32[4,3,256]{2,1,0:T(4,128)} copy(f32[4,3,256]{2,0,1:T(4,128)} %param.6) | data formatting | bytes 24576 | tf_op args[1]
  1.9 41.8 %steps.1 = (f32[512,256]{1,0:T(8,128)}, f32[13,256]{1,0:T(8,128)}) custom-call(f32[512,256]{1,0:T(8,128)} %f_ref.1, f32[4,3,256]{2,1,0:T(4,128)} %copy.6.n_ref, s32[4,256]{1,0:T(4,128)} %adj_ref.1, s32[1,2,256]{2,1,0:T(2,128)} %send_ref.1), custom_call_target="tpu_custom_call" | custom-call | tf_op jit(solution)/shard_map/steps/pallas_call | solution.py:652
  43.8 0.0 copy-start
  43.8 1.9 %copy.9 = f32[512,256]{1,0:T(8,128)} copy(f32[512,256]{1,0:T(8,128)} %get-tuple-element.4) | data formatting | bytes 1048576
  45.7 0.0 copy-done
  45.7 0.6 %copy.10 = f32[13,256]{1,0:T(8,128)} copy(f32[13,256]{1,0:T(8,128)S(1)} %copy-done) | data formatting | bytes 26624
Async XLA Ops:
  43.8 1.9 %copy-start = (f32[13,256]{1,0:T(8,128)S(1)}, f32[13,256]{1,0:T(8,128)}, u32[]{:S(2)}) copy-start(f32[13,256]{1,0:T(8,128)} %get-tuple-element.5) | copy-start | bytes 39940

commit v2 on v1

--- a/solution.py
+++ b/solution.py
@@ -382,14 +382,14 @@
     f_ref, n_ref, adj_ref, send_ref,
     out_ref, fields_ref,
     fx, nx, adjx, sendx, oh, tr0, fnew, tr1, phi_ref,
-    part0, rs0, zb0, full0, part1, rs1, zb1, full1,
+    qb0, zb0, total_mine, total_theirs, qb1, zb1, qb2, zb2,
     bulk_s, bulk_r, meta_s, meta_r,
-    a_s, a_r, b_s, b_r, c_s, c_r,
-    d_s, d_r, e_s, e_r, g_s, g_r,
+    a_s, a_r, b_s, b_r, x_s, x_r,
+    d_s, d_r, e_s, e_r, g_s, g_r, h_s, h_r,
 ):
     nodes, cells = f_ref.shape
     both = 2 * cells
-    faces = n_ref.shape[0]
+    faces = n_ref.shape[1]
     z_count = total_vel // (VXY * VXY)
     rows = nodes // CHUNKS
     group = lax.axis_index("space")
@@ -413,8 +413,7 @@
         pl.semaphore_signal(barrier, inc=1, device_id=at(group, me_z, q_of(step)), device_id_type=MESH)
     for step in range(1, ring):
         pl.semaphore_signal(barrier, inc=1, device_id=at(group, z_of(step), me_q), device_id_type=MESH)
-    for step in range(QUAD):
-        pl.semaphore_signal(barrier, inc=1, device_id=at(other, me_z, q_of(step)), device_id_type=MESH)
+    pl.semaphore_signal(barrier, inc=1, device_id=at(other, me_z, me_q), device_id_type=MESH)
 
     lane_v = node_velocity(lax.broadcasted_iota(jnp.int32, (1, nodes), 1) + vel * nodes, z_count)
     lx, ly, lz = lane_v
@@ -429,12 +428,9 @@
         phi = jnp.where(row_id == r, row, phi)
     phi_ref[...] = phi
     inv_total = 1.0 / total_vel
-    half = cells // 2
-    m_part = split_dot(phi, f_ref[...]) * inv_total
-    for q in range(QUAD):
-        part0[q] = m_part[(q // 2) * 8 : (q // 2) * 8 + 8, (q % 2) * half : (q % 2 + 1) * half]
-
-    pl.semaphore_wait(barrier, 2 * QUAD - 1 + ring - 1)
+    qb0[me_q] = split_dot(phi, f_ref[...]) * inv_total
+
+    pl.semaphore_wait(barrier, QUAD + ring - 1)
 
     def remote(src, dst, s, r, dev):
         return pltpu.make_async_remote_copy(
@@ -450,30 +446,38 @@
     for copy in metas:
         copy.start()
 
-    def scatter(part, rs, s, r):
+    def in_quad(buffer, s, r):
         copies = [
-            remote(part.at[q_of(t)], rs.at[t], s.at[t], r.at[t], at(group, me_z, q_of(t)))
+            remote(buffer.at[me_q], buffer.at[me_q], s.at[t], r.at[t], at(group, me_z, q_of(t)))
             for t in range(1, QUAD)
         ]
         for copy in copies:
             copy.start()
         return copies
 
-    def along_z(zb, s, r):
+    def along_z(buffer, s, r):
         copies = [
-            remote(zb.at[0], zb.at[t], s.at[t], r.at[t], at(group, z_of(t), me_q))
+            remote(buffer.at[me_z], buffer.at[me_z], s.at[t], r.at[t], at(group, z_of(t), me_q))
             for t in range(1, ring)
         ]
         for copy in copies:
             copy.start()
         return copies
 
+    def collect(copies, buffer, count):
+        for copy in copies:
+            copy.wait_recv()
+        result = buffer[0]
+        for t in range(1, count):
+            result = result + buffer[t]
+        return result
+
     def bulk(c):
         part = pl.ds(pl.multiple_of(c * rows, rows), rows)
         return remote(f_ref.at[part], fx.at[part], bulk_s.at[c], bulk_r.at[c], pair)
 
-    first = scatter(part0, rs0, a_s, a_r)
-    for c in range(CHUNKS):
+    first = in_quad(qb0, a_s, a_r)
+    for c in range(CHUNKS - 1):
         bulk(c).start()
 
     for copy in metas:
@@ -497,30 +501,8 @@
         index = jnp.concatenate([own, theirs], axis=1)
         oh[k] = (cell_id == index).astype(jnp.bfloat16)
 
-    for copy in first:
-        copy.wait_recv()
-    zb0[0] = part0[me_q] + rs0[1] + rs0[2] + rs0[3]
+    zb0[me_z] = collect(first, qb0, QUAD)
     second = along_z(zb0, b_s, b_r)
-    for copy in second:
-        copy.wait_recv()
-    total0 = zb0[0]
-    for t in range(1, ring):
-        total0 = total0 + zb0[t]
-    full0[0, me_q] = total0
-    third = []
-    for t in range(1, QUAD):
-        third.append(
-            remote(full0.at[0, me_q], full0.at[0, me_q], c_s.at[t], c_r.at[t], at(group, me_z, q_of(t)))
-        )
-    for t in range(QUAD):
-        third.append(
-            remote(
-                full0.at[0, me_q], full0.at[1, me_q], c_s.at[QUAD + t], c_r.at[QUAD + t],
-                at(other, me_z, q_of(t)),
-            )
-        )
-    for copy in third:
-        copy.start()
 
     def local_velocity(c, width):
         index = lax.broadcasted_iota(jnp.int32, (rows, width), 0) + (vel * nodes + c * rows)
@@ -538,9 +520,9 @@
             got = got[:rows] + got[rows:]
             normal = []
             for d in range(3):
-                line = n_ref[k, d : d + 1, :]
+                line = n_ref[d, k : k + 1, :]
                 if width > cells:
-                    line = jnp.concatenate([line, nx[k, d : d + 1, :]], axis=1)
+                    line = jnp.concatenate([line, nx[d, k : k + 1, :]], axis=1)
                 normal.append(line)
             speed = vx * normal[0] + vy * normal[1] + vz * normal[2]
             result = result + (jnp.maximum(speed, 0.0) * mine + jnp.minimum(speed, 0.0) * got)
@@ -556,23 +538,25 @@
         tr0[part, :] = transport(state, c, both)
         return carry
 
-    early = CHUNKS // 2
-    lax.fori_loop(0, early, first_transport, 0)
-    for copy in third:
-        copy.wait_recv()
-
-    def joined(full):
-        top = jnp.concatenate([full[0], full[1]], axis=1)
-        bottom = jnp.concatenate([full[2], full[3]], axis=1)
-        return jnp.concatenate([top, bottom], axis=0)
-
-    mom0 = jnp.concatenate([joined(full0[0]), joined(full0[1])], axis=1)
-    fields0, quad0, freq0 = coefficient_rows(mom0)
-    z0 = gauss_total(quad0, both, z_count) * inv_total
-    gain0 = time_step * freq0 * fields0[0] / z0
-    keep0 = 1.0 - time_step * freq0
-
-    lax.fori_loop(early, CHUNKS, first_transport, 0)
+    lax.fori_loop(0, 1, first_transport, 0)
+    total_mine[...] = collect(second, zb0, ring)
+    third = [remote(total_mine, total_theirs, x_s, x_r, pair)]
+    third[0].start()
+    bulk(CHUNKS - 1).start()
+
+    def step_rows(moments):
+        fields, quad, freq = coefficient_rows(moments)
+        norm = gauss_total(quad, cells, z_count) * inv_total
+        return quad, time_step * freq * fields[0] / norm, 1.0 - time_step * freq
+
+    own_quad, own_gain, own_keep = step_rows(total_mine[...])
+    lax.fori_loop(1, CHUNKS - 1, first_transport, 0)
+    third[0].wait_recv()
+    their_quad, their_gain, their_keep = step_rows(total_theirs[...])
+    quad0 = [jnp.concatenate([a, b], axis=1) for a, b in zip(own_quad, their_quad)]
+    gain0 = jnp.concatenate([own_gain, their_gain], axis=1)
+    keep0 = jnp.concatenate([own_keep, their_keep], axis=1)
+    lax.fori_loop(CHUNKS - 1, CHUNKS, first_transport, 0)
 
     def second_transport(c, carry):
         part, state = wide(c)
@@ -585,32 +569,15 @@
     lax.fori_loop(0, CHUNKS, second_transport, 0)
 
     phi = phi_ref[...]
-    m_new = split_dot(phi, fnew[...]) * inv_total
-    m_tr = split_dot(phi, tr1[...]) * inv_total
-    for q in range(QUAD):
-        src = m_new if q < 2 else m_tr
-        part1[q] = src[:, (q % 2) * half : (q % 2 + 1) * half]
-    fourth = scatter(part1, rs1, d_s, d_r)
-    for copy in fourth:
-        copy.wait_recv()
-    zb1[0] = part1[me_q] + rs1[1] + rs1[2] + rs1[3]
-    fifth = along_z(zb1, e_s, e_r)
-    for copy in fifth:
-        copy.wait_recv()
-    total1 = zb1[0]
-    for t in range(1, ring):
-        total1 = total1 + zb1[t]
-    full1[me_q] = total1
-    sixth = [
-        remote(full1.at[me_q], full1.at[me_q], g_s.at[t], g_r.at[t], at(group, me_z, q_of(t)))
-        for t in range(1, QUAD)
-    ]
-    for copy in sixth:
-        copy.start()
-    for copy in sixth:
-        copy.wait_recv()
-    mom1 = jnp.concatenate([full1[0], full1[1]], axis=1)
-    mom_t = jnp.concatenate([full1[2], full1[3]], axis=1)
+    qb1[me_q] = split_dot(phi, fnew[...]) * inv_total
+    fourth = in_quad(qb1, d_s, d_r)
+    qb2[me_q] = split_dot(phi, tr1[...]) * inv_total
+    fifth = in_quad(qb2, e_s, e_r)
+    zb1[me_z] = collect(fourth, qb1, QUAD)
+    sixth = along_z(zb1, g_s, g_r)
+    zb2[me_z] = collect(fifth, qb2, QUAD)
+    seventh = along_z(zb2, h_s, h_r)
+    mom1 = collect(sixth, zb1, ring)
     fields1, quad1, freq1 = coefficient_rows(mom1)
     sums = gauss_moments(quad1, cells, z_count)
     inv_sum = 1.0 / sums[0]
@@ -628,6 +595,7 @@
         return carry
 
     lax.fori_loop(0, CHUNKS, finish, 0)
+    mom_t = collect(seventh, zb2, ring)
     ratio = lift * inv_sum
     last = [
         keep1 * mom1[r : r + 1] - time_step * mom_t[r : r + 1] + ratio * sums[r] for r in range(13)
@@ -637,15 +605,15 @@
         fields_ref[r : r + 1, :] = final[r]
     for c in range(CHUNKS):
         bulk(c).wait_send()
-    for copy in metas + first + second + third + fourth + fifth + sixth:
+    for copy in metas + first + second + third + fourth + fifth + sixth + seventh:
         copy.wait_send()
 
 
 def per_device_pair(distribution, normals, adjacency, send_list, block_counts):
     nodes, cells = distribution.shape
+    normals = normals.transpose(1, 0, 2)
     size = lax.axis_size("vel")
     ring = size // QUAD
-    half = cells // 2
     f32 = jnp.float32
     dma = pltpu.SemaphoreType.DMA
     vmem = pl.BlockSpec(memory_space=pltpu.VMEM)
@@ -662,22 +630,23 @@
             pltpu.VMEM(normals.shape, f32),
             pltpu.VMEM(adjacency.shape, jnp.int32),
             pltpu.VMEM(send_list.shape, jnp.int32),
-            pltpu.VMEM((normals.shape[0], 2 * cells, 2 * cells), jnp.bfloat16),
+            pltpu.VMEM((normals.shape[1], 2 * cells, 2 * cells), jnp.bfloat16),
             pltpu.VMEM((nodes, 2 * cells), f32),
             pltpu.VMEM((nodes, cells), f32),
             pltpu.VMEM((nodes, cells), f32),
             pltpu.VMEM((16, nodes), f32),
-            pltpu.VMEM((QUAD, 8, half), f32),
-            pltpu.VMEM((QUAD, 8, half), f32),
-            pltpu.VMEM((ring, 8, half), f32),
-            pltpu.VMEM((2, QUAD, 8, half), f32),
-            pltpu.VMEM((QUAD, 16, half), f32),
-            pltpu.VMEM((QUAD, 16, half), f32),
-            pltpu.VMEM((ring, 16, half), f32),
-            pltpu.VMEM((QUAD, 16, half), f32),
+            pltpu.VMEM((QUAD, 16, cells), f32),
+            pltpu.VMEM((ring, 16, cells), f32),
+            pltpu.VMEM((16, cells), f32),
+            pltpu.VMEM((16, cells), f32),
+            pltpu.VMEM((QUAD, 16, cells), f32),
+            pltpu.VMEM((ring, 16, cells), f32),
+            pltpu.VMEM((QUAD, 16, cells), f32),
+            pltpu.VMEM((ring, 16, cells), f32),
             dma((CHUNKS,)), dma((CHUNKS,)), dma((3,)), dma((3,)),
-            dma((QUAD,)), dma((QUAD,)), dma((ring,)), dma((ring,)), dma((2 * QUAD,)), dma((2 * QUAD,)),
-            dma((QUAD,)), dma((QUAD,)), dma((ring,)), dma((ring,)), dma((QUAD,)), dma((QUAD,)),
+            dma((QUAD,)), dma((QUAD,)), dma((ring,)), dma((ring,)), dma, dma,
+            dma((QUAD,)), dma((QUAD,)), dma((QUAD,)), dma((QUAD,)),
+            dma((ring,)), dma((ring,)), dma((ring,)), dma((ring,)),
         ],
         compiler_params=pltpu.CompilerParams(collective_id=0, has_side_effects=True),
         name="steps",

time: 46.5 us -> 38.8 us (0.83)
  Pallas kernels: 41.8 us -> 35.5 us
  local copies, waits for them, and re-layouts: 3.8 us -> 2.48 us
    pallas_call x1, Pallas kernels: 41.8 us -> 35.5 us  [per_device_pair(): pl.pallas_call(functools.partial(step_kernel, nodes * size), out_shape=(j...]
    unnamed x5 -> x4, local copies, waits for them, and re-layouts: 3.8 us -> 2.48 us
where the time goes in v2:
time: 38.8 us; the launch traced here: 38.7 us
  Pallas kernels  35.5 us (91%)
  local copies, waits for them, and re-layouts  2.48 us (6%)
  between operations  0.65 us (2%)
    pallas_call x1, Pallas kernels, per_device_pair(): pl.pallas_call(functools.partial(step_kernel, nodes * size), out_shape=(j...  35.5 us
    unnamed x4, local copies, waits for them, and re-layouts  2.48 us

profile of v2, /device:TPU:0, one launch (start us, length us, event | category | flops | bytes accessed | tf_op | source)
XLA Modules:
  0.0 38.7 jit_solution(4678570174411249978)
XLA Ops:
  0.6 35.5 %steps.1 = (f32[512,256]{1,0:T(8,128)}, f32[13,256]{1,0:T(8,128)}) custom-call(f32[512,256]{1,0:T(8,128)} %f_ref.1, f32[3,4,256]{2,1,0:T(4,128)} %bitcast.1, s32[4,256]{1,0:T(4,128)} %adj_ref.1, s32[1,2,256]{2,1,0:T(2,128)} %send_ref.1), custom_call_target="tpu_custom_call" | custom-call | tf_op jit(solution)/shard_map/steps/pallas_call | solution.py:620
  36.2 0.0 copy-start
  36.2 1.9 %copy.8 = f32[512,256]{1,0:T(8,128)} copy(f32[512,256]{1,0:T(8,128)} %get-tuple-element.4) | data formatting | bytes 1048576
  38.1 0.0 copy-done
  38.1 0.6 %copy.9 = f32[13,256]{1,0:T(8,128)} copy(f32[13,256]{1,0:T(8,128)S(1)} %copy-done) | data formatting | bytes 26624
Async XLA Ops:
  36.2 1.9 %copy-start = (f32[13,256]{1,0:T(8,128)S(1)}, f32[13,256]{1,0:T(8,128)}, u32[]{:S(2)}) copy-start(f32[13,256]{1,0:T(8,128)} %get-tuple-element.5) | copy-start | bytes 39940

commit v3 on v2

--- a/solution.py
+++ b/solution.py
@@ -241,11 +241,13 @@
 LOG2E = 1.4426950408889634
 QUAD = 4
 CHUNKS = 4
+PIECES = 8
+HELD = 3
 HI = lax.Precision.HIGHEST
 
 
 def coefficient_rows(m):
-    full = macroscopic_rows([m[r : r + 1, :] for r in range(13)])
+    full = macroscopic_rows(m)
     scale = -0.5 * LOG2E
     return full[:13], [row * scale for row in full[13:23]], full[23]
 
@@ -379,15 +381,15 @@
 
 def step_kernel(
     total_vel,
-    f_ref, n_ref, adj_ref, send_ref,
-    out_ref, fields_ref,
-    fx, nx, adjx, sendx, oh, tr0, fnew, tr1, phi_ref,
+    f_hbm, n_ref, adj_ref, send_ref,
+    out_hbm, fields_ref,
+    f_ref, out_ref, load_s, store_s, fx, nx, adjx, sendx, oh, tr0, fnew, tr1, phi_ref,
     qb0, zb0, total_mine, total_theirs, qb1, zb1, qb2, zb2,
     bulk_s, bulk_r, meta_s, meta_r,
     a_s, a_r, b_s, b_r, x_s, x_r,
     d_s, d_r, e_s, e_r, g_s, g_r, h_s, h_r,
 ):
-    nodes, cells = f_ref.shape
+    nodes, cells = f_hbm.shape
     both = 2 * cells
     faces = n_ref.shape[1]
     z_count = total_vel // (VXY * VXY)
@@ -414,6 +416,9 @@
     for step in range(1, ring):
         pl.semaphore_signal(barrier, inc=1, device_id=at(group, z_of(step), me_q), device_id_type=MESH)
     pl.semaphore_signal(barrier, inc=1, device_id=at(other, me_z, me_q), device_id_type=MESH)
+
+    load = pltpu.make_async_copy(f_hbm, f_ref, load_s)
+    load.start()
 
     lane_v = node_velocity(lax.broadcasted_iota(jnp.int32, (1, nodes), 1) + vel * nodes, z_count)
     lx, ly, lz = lane_v
@@ -428,6 +433,7 @@
         phi = jnp.where(row_id == r, row, phi)
     phi_ref[...] = phi
     inv_total = 1.0 / total_vel
+    load.wait()
     qb0[me_q] = split_dot(phi, f_ref[...]) * inv_total
 
     pl.semaphore_wait(barrier, QUAD + ring - 1)
@@ -472,12 +478,15 @@
             result = result + buffer[t]
         return result
 
+    piece = nodes // PIECES
+    ratio = PIECES // CHUNKS
+
     def bulk(c):
-        part = pl.ds(pl.multiple_of(c * rows, rows), rows)
+        part = pl.ds(pl.multiple_of(c * piece, piece), piece)
         return remote(f_ref.at[part], fx.at[part], bulk_s.at[c], bulk_r.at[c], pair)
 
     first = in_quad(qb0, a_s, a_r)
-    for c in range(CHUNKS - 1):
+    for c in range(PIECES - HELD):
         bulk(c).start()
 
     for copy in metas:
@@ -533,30 +542,43 @@
         return part, jnp.concatenate([f_ref[part, :], fx[part, :]], axis=1)
 
     def first_transport(c, carry):
-        bulk(c).wait_recv()
+        for t in range(ratio):
+            bulk(c * ratio + t).wait_recv()
         part, state = wide(c)
         tr0[part, :] = transport(state, c, both)
         return carry
 
-    lax.fori_loop(0, 1, first_transport, 0)
+    lax.fori_loop(0, CHUNKS // 2, first_transport, 0)
     total_mine[...] = collect(second, zb0, ring)
     third = [remote(total_mine, total_theirs, x_s, x_r, pair)]
     third[0].start()
-    bulk(CHUNKS - 1).start()
-
-    def step_rows(moments):
-        fields, quad, freq = coefficient_rows(moments)
-        norm = gauss_total(quad, cells, z_count) * inv_total
-        return quad, time_step * freq * fields[0] / norm, 1.0 - time_step * freq
-
-    own_quad, own_gain, own_keep = step_rows(total_mine[...])
-    lax.fori_loop(1, CHUNKS - 1, first_transport, 0)
+    for c in range(PIECES - HELD, PIECES):
+        bulk(c).start()
+
+    def rows_of(moments):
+        return [moments[r : r + 1] for r in range(13)]
+
+    mom0 = rows_of(total_mine[...])
+    fields0, own_quad, freq0 = coefficient_rows(mom0)
+    sums0 = gauss_moments(own_quad, cells, z_count)
+    lift0 = time_step * freq0 * fields0[0] / sums0[0]
+    own_gain = lift0 * float(total_vel)
+    own_keep = 1.0 - time_step * freq0
+    lax.fori_loop(CHUNKS // 2, CHUNKS - 1, first_transport, 0)
     third[0].wait_recv()
-    their_quad, their_gain, their_keep = step_rows(total_theirs[...])
+    fields_x, their_quad, freq_x = coefficient_rows(rows_of(total_theirs[...]))
+    norm_x = gauss_total(their_quad, cells, z_count) * inv_total
+    their_gain = time_step * freq_x * fields_x[0] / norm_x
+    their_keep = 1.0 - time_step * freq_x
     quad0 = [jnp.concatenate([a, b], axis=1) for a, b in zip(own_quad, their_quad)]
     gain0 = jnp.concatenate([own_gain, their_gain], axis=1)
     keep0 = jnp.concatenate([own_keep, their_keep], axis=1)
+    ahead = nodes - rows
+    phi = phi_ref[...]
+    m_t0 = split_dot(phi[:, :ahead], tr0[:ahead, :cells])
     lax.fori_loop(CHUNKS - 1, CHUNKS, first_transport, 0)
+    qb1[me_q] = (m_t0 + split_dot(phi[:, ahead:], tr0[ahead:, :cells])) * inv_total
+    fourth = in_quad(qb1, d_s, d_r)
 
     def second_transport(c, carry):
         part, state = wide(c)
@@ -566,24 +588,28 @@
         tr1[part, :] = transport(state, c, cells)
         return carry
 
-    lax.fori_loop(0, CHUNKS, second_transport, 0)
-
-    phi = phi_ref[...]
-    qb1[me_q] = split_dot(phi, fnew[...]) * inv_total
-    fourth = in_quad(qb1, d_s, d_r)
+    lax.fori_loop(0, CHUNKS // 2, second_transport, 0)
+    zb1[me_z] = collect(fourth, qb1, QUAD)
+    sixth = along_z(zb1, g_s, g_r)
+    lax.fori_loop(CHUNKS // 2, CHUNKS, second_transport, 0)
     qb2[me_q] = split_dot(phi, tr1[...]) * inv_total
     fifth = in_quad(qb2, e_s, e_r)
-    zb1[me_z] = collect(fourth, qb1, QUAD)
-    sixth = along_z(zb1, g_s, g_r)
     zb2[me_z] = collect(fifth, qb2, QUAD)
     seventh = along_z(zb2, h_s, h_r)
-    mom1 = collect(sixth, zb1, ring)
+    mom_t0 = collect(sixth, zb1, ring)
+    mom1 = [
+        own_keep * mom0[r] - time_step * mom_t0[r : r + 1] + lift0 * sums0[r] for r in range(13)
+    ]
     fields1, quad1, freq1 = coefficient_rows(mom1)
     sums = gauss_moments(quad1, cells, z_count)
     inv_sum = 1.0 / sums[0]
     lift = time_step * freq1 * fields1[0]
     gain1 = lift * inv_sum * float(total_vel)
     keep1 = 1.0 - time_step * freq1
+
+    def store(c):
+        part = pl.ds(pl.multiple_of(c * rows, rows), rows)
+        return pltpu.make_async_copy(out_ref.at[part], out_hbm.at[part], store_s.at[c])
 
     def finish(c, carry):
         part = pl.ds(pl.multiple_of(c * rows, rows), rows)
@@ -592,18 +618,21 @@
             keep1 * fnew[part, :] - time_step * tr1[part, :]
             + gain1 * jnp.exp2(exponent_at(quad1, vx, vy, vz))
         )
+        store(c).start()
         return carry
 
     lax.fori_loop(0, CHUNKS, finish, 0)
     mom_t = collect(seventh, zb2, ring)
-    ratio = lift * inv_sum
+    slope = lift * inv_sum
     last = [
-        keep1 * mom1[r : r + 1] - time_step * mom_t[r : r + 1] + ratio * sums[r] for r in range(13)
+        keep1 * mom1[r] - time_step * mom_t[r : r + 1] + slope * sums[r] for r in range(13)
     ]
     final = macroscopic_rows(last)
     for r in range(13):
         fields_ref[r : r + 1, :] = final[r]
     for c in range(CHUNKS):
+        store(c).wait()
+    for c in range(PIECES):
         bulk(c).wait_send()
     for copy in metas + first + second + third + fourth + fifth + sixth + seventh:
         copy.wait_send()
@@ -617,15 +646,20 @@
     f32 = jnp.float32
     dma = pltpu.SemaphoreType.DMA
     vmem = pl.BlockSpec(memory_space=pltpu.VMEM)
+    anywhere = pl.BlockSpec(memory_space=pl.ANY)
     return pl.pallas_call(
         functools.partial(step_kernel, nodes * size),
         out_shape=(
             jax.ShapeDtypeStruct((nodes, cells), f32),
             jax.ShapeDtypeStruct((13, cells), f32),
         ),
-        in_specs=[vmem] * 4,
-        out_specs=(vmem, vmem),
+        in_specs=[anywhere] + [vmem] * 3,
+        out_specs=(anywhere, vmem),
         scratch_shapes=[
+            pltpu.VMEM((nodes, cells), f32),
+            pltpu.VMEM((nodes, cells), f32),
+            dma,
+            dma((CHUNKS,)),
             pltpu.VMEM((nodes, cells), f32),
             pltpu.VMEM(normals.shape, f32),
             pltpu.VMEM(adjacency.shape, jnp.int32),
@@ -643,7 +677,7 @@
             pltpu.VMEM((ring, 16, cells), f32),
             pltpu.VMEM((QUAD, 16, cells), f32),
             pltpu.VMEM((ring, 16, cells), f32),
-            dma((CHUNKS,)), dma((CHUNKS,)), dma((3,)), dma((3,)),
+            dma((PIECES,)), dma((PIECES,)), dma((3,)), dma((3,)),
             dma((QUAD,)), dma((QUAD,)), dma((ring,)), dma((ring,)), dma, dma,
             dma((QUAD,)), dma((QUAD,)), dma((QUAD,)), dma((QUAD,)),
             dma((ring,)), dma((ring,)), dma((ring,)), dma((ring,)),

time: 38.8 us -> 38 us (0.979)
  Pallas kernels: 35.5 us -> 34.6 us
    pallas_call x1, Pallas kernels: 35.5 us -> 34.6 us  [per_device_pair(): pl.pallas_call(functools.partial(step_kernel, nodes * size), out_shape=(j...]
where the time goes in v3:
time: 38 us; the launch traced here: 37.7 us
  Pallas kernels  34.6 us (91%)
  local copies, waits for them, and re-layouts  2.48 us (7%)
  between operations  0.65 us (2%)
    pallas_call x1, Pallas kernels, per_device_pair(): pl.pallas_call(functools.partial(step_kernel, nodes * size), out_shape=(j...  34.6 us
    unnamed x4, local copies, waits for them, and re-layouts  2.48 us

profile of v3, /device:TPU:0, one launch (start us, length us, event | category | flops | bytes accessed | tf_op | source)
XLA Modules:
  0.0 37.7 jit_solution(4179119007834341021)
XLA Ops:
  0.6 34.6 %steps.1 = (f32[512,256]{1,0:T(8,128)}, f32[13,256]{1,0:T(8,128)}) custom-call(f32[512,256]{1,0:T(8,128)} %f_hbm.1, f32[3,4,256]{2,1,0:T(4,128)} %bitcast.1, s32[4,256]{1,0:T(4,128)} %adj_ref.1, s32[1,2,256]{2,1,0:T(2,128)} %send_ref.1), custom_call_target="tpu_custom_call" | custom-call | tf_op jit(solution)/shard_map/steps/pallas_call | solution.py:650
  35.3 0.0 copy-start
  35.3 1.9 %copy.8 = f32[512,256]{1,0:T(8,128)} copy(f32[512,256]{1,0:T(8,128)} %get-tuple-element.4) | data formatting | bytes 1048576
  37.1 0.0 copy-done
  37.1 0.6 %copy.9 = f32[13,256]{1,0:T(8,128)} copy(f32[13,256]{1,0:T(8,128)S(1)} %copy-done) | data formatting | bytes 26624
Async XLA Ops:
  35.3 1.9 %copy-start = (f32[13,256]{1,0:T(8,128)S(1)}, f32[13,256]{1,0:T(8,128)}, u32[]{:S(2)}) copy-start(f32[13,256]{1,0:T(8,128)} %get-tuple-element.5) | copy-start | bytes 39940

commit v4 on v3

--- a/solution.py
+++ b/solution.py
@@ -548,7 +548,7 @@
         tr0[part, :] = transport(state, c, both)
         return carry
 
-    lax.fori_loop(0, CHUNKS // 2, first_transport, 0)
+    lax.fori_loop(0, 1, first_transport, 0)
     total_mine[...] = collect(second, zb0, ring)
     third = [remote(total_mine, total_theirs, x_s, x_r, pair)]
     third[0].start()
@@ -564,7 +564,7 @@
     lift0 = time_step * freq0 * fields0[0] / sums0[0]
     own_gain = lift0 * float(total_vel)
     own_keep = 1.0 - time_step * freq0
-    lax.fori_loop(CHUNKS // 2, CHUNKS - 1, first_transport, 0)
+    lax.fori_loop(1, CHUNKS - 1, first_transport, 0)
     third[0].wait_recv()
     fields_x, their_quad, freq_x = coefficient_rows(rows_of(total_theirs[...]))
     norm_x = gauss_total(their_quad, cells, z_count) * inv_total
@@ -588,10 +588,10 @@
         tr1[part, :] = transport(state, c, cells)
         return carry
 
-    lax.fori_loop(0, CHUNKS // 2, second_transport, 0)
+    lax.fori_loop(0, CHUNKS - 1, second_transport, 0)
     zb1[me_z] = collect(fourth, qb1, QUAD)
     sixth = along_z(zb1, g_s, g_r)
-    lax.fori_loop(CHUNKS // 2, CHUNKS, second_transport, 0)
+    lax.fori_loop(CHUNKS - 1, CHUNKS, second_transport, 0)
     qb2[me_q] = split_dot(phi, tr1[...]) * inv_total
     fifth = in_quad(qb2, e_s, e_r)
     zb2[me_z] = collect(fifth, qb2, QUAD)

time: 38 us -> 37.2 us (0.979)
  Pallas kernels: 34.6 us -> 33.8 us
    pallas_call x1, Pallas kernels: 34.6 us -> 33.8 us  [per_device_pair(): pl.pallas_call(functools.partial(step_kernel, nodes * size), out_shape=(j...]
where the time goes in v4:
time: 37.2 us; the launch traced here: 37 us
  Pallas kernels  33.8 us (91%)
  local copies, waits for them, and re-layouts  2.48 us (7%)
  between operations  0.65 us (2%)
    pallas_call x1, Pallas kernels, per_device_pair(): pl.pallas_call(functools.partial(step_kernel, nodes * size), out_shape=(j...  33.8 us
    unnamed x4, local copies, waits for them, and re-layouts  2.48 us

profile of v4, /device:TPU:0, one launch (start us, length us, event | category | flops | bytes accessed | tf_op | source)
XLA Modules:
  0.0 37.0 jit_solution(663749584196880694)
XLA Ops:
  0.6 33.8 %steps.1 = (f32[512,256]{1,0:T(8,128)}, f32[13,256]{1,0:T(8,128)}) custom-call(f32[512,256]{1,0:T(8,128)} %f_hbm.1, f32[3,4,256]{2,1,0:T(4,128)} %bitcast.1, s32[4,256]{1,0:T(4,128)} %adj_ref.1, s32[1,2,256]{2,1,0:T(2,128)} %send_ref.1), custom_call_target="tpu_custom_call" | custom-call | tf_op jit(solution)/shard_map/steps/pallas_call | solution.py:650
  34.5 0.0 copy-start
  34.5 1.9 %copy.8 = f32[512,256]{1,0:T(8,128)} copy(f32[512,256]{1,0:T(8,128)} %get-tuple-element.4) | data formatting | bytes 1048576
  36.4 0.0 copy-done
  36.4 0.6 %copy.9 = f32[13,256]{1,0:T(8,128)} copy(f32[13,256]{1,0:T(8,128)S(1)} %copy-done) | data formatting | bytes 26624
Async XLA Ops:
  34.5 1.9 %copy-start = (f32[13,256]{1,0:T(8,128)S(1)}, f32[13,256]{1,0:T(8,128)}, u32[]{:S(2)}) copy-start(f32[13,256]{1,0:T(8,128)} %get-tuple-element.5) | copy-start | bytes 39940
